TPU v7x, 32 devices: a whole 2x2x4 slice. The times are simulated.
32 devices in a mesh: dp: 4 (over y, x), depth: 4 (over z), grid: 2 (over core).
Axes of the slice: x: 2, y: 2, z: 4, core: 2. Of those that a mesh axis runs over, the one named last changes fastest.
Arguments:
- tokens: bfloat16 [1024, 12288], P(('dp', 'depth'), 'grid'), may hold values from -6 to 6
- weight: bfloat16 [12288, 24576], P('grid', 'depth'), may hold values from -0.0546875 to 0.0546875
- cotangent: bfloat16 [1024, 24576], P(('dp', 'grid'), 'depth'), may hold values from -0.5 to 0.5
Outputs:
- hidden: bfloat16 [1024, 24576], P(('dp', 'grid'), 'depth')
- weight_grad: bfloat16 [12288, 24576], P(('grid', 'dp'), 'depth')
All inputs are finite; a program needn't handle non-finite values.
Results may differ from a plain program's by a relative error of at most 0.011.
Values may be sent and summed in bfloat16 or wider, within the bound.
No kernel may reach another device: no remote copies, remote signals or barrier semaphores. Data moves between devices by JAX's collectives and lax.ppermute only.
A program may use at most 192 MiB of HBM per device.

v0:
```python
import jax
import jax.numpy as jnp
from jax import lax
from jax.sharding import PartitionSpec as P


def gelu_tanh(values):
    return jax.nn.gelu(values, approximate=True)


def transposed_product(left, right):
    return lax.dot_general(
        left, right, (((0,), (0,)), ((), ())), preferred_element_type=jnp.float32
    )


def local(tokens, weight, cotangent):
    all_rows = lax.all_gather(tokens, ("dp", "depth"), axis=0, tiled=True)
    group_size = all_rows.shape[0] // lax.axis_size("dp")
    own_rows = lax.dynamic_slice_in_dim(all_rows, lax.axis_index("dp") * group_size, group_size, 0)
    partial_pre = jnp.dot(own_rows, weight, preferred_element_type=jnp.float32)
    preact = lax.psum_scatter(partial_pre, "grid", scatter_dimension=0, tiled=True)
    activated, pullback = jax.vjp(gelu_tanh, preact)
    hidden = activated.astype(jnp.bfloat16)
    grad_pre = pullback(cotangent.astype(jnp.float32))[0].astype(jnp.bfloat16)
    sub_width = all_rows.shape[1] // lax.axis_size("dp")
    columns = lax.dynamic_slice_in_dim(all_rows, lax.axis_index("dp") * sub_width, sub_width, 1)
    weight_grad = transposed_product(
        columns, lax.all_gather(grad_pre, ("dp", "grid"), axis=0, tiled=True)
    )
    return (hidden, weight_grad.astype(jnp.bfloat16))


def solution(mesh):
    return jax.shard_map(
        local,
        mesh=mesh,
        in_specs=(P(("dp", "depth"), "grid"), P("grid", "depth"), P(("dp", "grid"), "depth")),
        out_specs=(P(("dp", "grid"), "depth"), P(("grid", "dp"), "depth")),
        check_vma=False,
    )
```

profile of v0, /device:TPU:0, one launch (start us, length us, event | category | flops | bytes accessed | tf_op | source)
XLA Modules:
  0.0 322.6 jit_solution(14169711380635420403)
XLA Ops:
  7.2 0.0 all-gather.3.cloned.1.call-start
  7.2 0.7 all-gather.3.cloned.1.call-update
  7.9 0.0 reduce-scatter.2.cloned.1.call-start
  7.9 157.1 %all-gather.3.cloned.1.call-done = bf16[1024,6144]{1,0:T(8,128)(2,1)} async-done(((bf16[64,6144]{1,0:T(8,128)(2,1)}), bf16[1024,6144]{1,0:T(8,128)(2,1)}) %all-gather.3.cloned.1.call-update) | async-done | bytes 12582928 | tf_op jit(solution)/shard_map/all_gather | solution.py:18
  165.0 31.6 %fusion.11 = f32[256,6144]{1,0:T(8,128)} fusion(bf16[6144,6144]{1,0:T(8,128)(2,1)} %param.4, bf16[1024,6144]{1,0:T(8,128)(2,1)} %all-gather.3.cloned.1.call-done, s32[]{:T(128)S(6)} %select_n.6), kind=kOutput, calls=%fused_computation.17 | convolution fusion | flops 19327352832 | bytes 84934656 | tf_op jit(solution)/shard_map/dot_general | solution.py:21
  196.6 0.0 copy-start
  196.6 0.0 reduce-scatter.2.cloned.1.call-update
  196.6 0.0 all-gather.5.cloned.1.call-start
  196.7 12.3 %reduce-scatter.2.cloned.1.call-done = f32[128,6144]{1,0:T(8,128)} async-done(((f32[256,6144]{1,0:T(8,128)}), f32[128,6144]{1,0:T(8,128)}) %reduce-scatter.2.cloned.1.call-update) | async-done | bytes 3145744 | tf_op jit(solution)/shard_map/reduce_scatter | solution.py:22
  209.0 0.0 copy-done
  209.0 4.9 %fusion.2 = (bf16[128,6144]{1,0:T(8,128)(2,1)}, bf16[128,6144]{1,0:T(8,128)(2,1)}) fusion(bf16[128,6144]{1,0:T(8,128)(2,1)S(1)} %copy-done, f32[128,6144]{1,0:T(8,128)} %reduce-scatter.2.cloned.1.call-done), kind=kLoop, calls=%fused_computation.7 | loop fusion | flops 18087936 | bytes 7864320 | tf_op jit(solution)/shard_map/convert_element_type | solution.py:25
  213.9 0.0 all-gather.5.cloned.1.call-update
  214.0 74.2 %all-gather.5.cloned.1.call-done = bf16[1024,6144]{1,0:T(8,128)(2,1)} async-done(((bf16[128,6144]{1,0:T(8,128)(2,1)}), bf16[1024,6144]{1,0:T(8,128)(2,1)}) %all-gather.5.cloned.1.call-update) | async-done | bytes 12582928 | tf_op jit(solution)/shard_map/all_gather | solution.py:29
  288.1 27.9 %convolution_convert_fusion = bf16[1536,6144]{1,0:T(8,128)(2,1)} fusion(bf16[1024,6144]{1,0:T(8,128)(2,1)} %all-gather.5.cloned.1.call-done, bf16[1024,6144]{1,0:T(8,128)(2,1)} %all-gather.3.cloned.1.call-done, s32[]{:T(128)S(6)} %select_n.7), kind=kOutput, calls=%fused_computation | convolution fusion | flops 19336790016 | bytes 34603012 | tf_op jit(solution)/shard_map/dot_general | solution.py:12
Async XLA Ops:
  7.2 157.8 %all-gather.3.cloned.1.call-start = ((), (), s32[]{:S(2)}) async-start(), calls=%async_computation.1 | async-start | bytes 13369344 | tf_op jit(solution)/shard_map/all_gather | solution.py:18
  7.9 201.1 %reduce-scatter.2.cloned.1.call-start = ((), (), s32[]{:S(2)}) async-start(), calls=%async_computation.2 | async-start | bytes 9437184 | tf_op jit(solution)/shard_map/reduce_scatter | solution.py:22
  196.6 12.4 %copy-start = (bf16[128,6144]{1,0:T(8,128)(2,1)S(1)}, bf16[128,6144]{1,0:T(8,128)(2,1)}, u32[]{:S(2)}) copy-start(bf16[128,6144]{1,0:T(8,128)(2,1)} %param.5) | copy-start | bytes 4718596
  196.6 91.5 %all-gather.5.cloned.1.call-start = ((), (), s32[]{:S(2)}) async-start(), calls=%async_computation.3 | async-start | bytes 14155776 | tf_op jit(solution)/shard_map/all_gather | solution.py:29
Sparse Core Ops, SparseCore 0:
  10.8 154.1 all-gather.2
  196.8 12.2 reduce-scatter.1
  214.1 73.9 all-gather.4
where the time goes:
time: 323 us
  waiting for transfers between devices  244 us (76%)
  matrix products  59.5 us (18%)
  between operations  13.8 us (4%)
  other arithmetic  4.9 us (2%)
    all_gather x1, waiting for transfers between devices, local(): all_rows = lax.all_gather(tokens, ('dp', 'depth'), axis=0, tiled=True)  157 us
    all_gather x1, waiting for transfers between devices, local(): lax.all_gather(grad_pre, ('dp', 'grid'), axis=0, tiled=True)  74.2 us
    dot_general x1, matrix products, local(): partial_pre = jnp.dot(own_rows, weight, preferred_element_type=jnp.float32)  31.6 us
    dot_general x1, matrix products, transposed_product(): lax.dot_general(left, right, (((0,), (0,)), ((), ())), preferred_element_...  27.9 us
    reduce_scatter x1, waiting for transfers between devices, local(): lax.psum_scatter(partial_pre, 'grid', scatter_dimension=0, tiled=True)  12.3 us
  transfers between devices with their start and end apart: 3, of which 3 were waited for; matrix products, arithmetic and copies ran while one was open for 0% of the time, Pallas kernels for 0%

commit v1 on v0

--- a/solution.py
+++ b/solution.py
@@ -2,6 +2,12 @@
 import jax.numpy as jnp
 from jax import lax
 from jax.sharding import PartitionSpec as P
+
+
+def tiled_gather(x, axis, dim):
+    size = lax.axis_size(axis)
+    repeats = [size if d == dim else 1 for d in range(x.ndim)]
+    return lax.all_to_all(jnp.tile(x, repeats), axis, split_axis=dim, concat_axis=dim, tiled=True)
 
 
 def gelu_tanh(values):
@@ -15,7 +21,7 @@
 
 
 def local(tokens, weight, cotangent):
-    all_rows = lax.all_gather(tokens, ("dp", "depth"), axis=0, tiled=True)
+    all_rows = tiled_gather(tokens, ("dp", "depth"), 0)
     group_size = all_rows.shape[0] // lax.axis_size("dp")
     own_rows = lax.dynamic_slice_in_dim(all_rows, lax.axis_index("dp") * group_size, group_size, 0)
     partial_pre = jnp.dot(own_rows, weight, preferred_element_type=jnp.float32)

time: 323 us -> 475 us (1.47)
  waiting for transfers between devices: 244 us -> 380 us
  starting transfers between devices: 0.12 us -> 8.65 us
  local copies, waits for them, and re-layouts: 0.01 us -> 7.54 us
    all_to_all x0 -> x1, waiting for transfers between devices: none -> 296 us  [tiled_gather(): lax.all_to_all(jnp.tile(x, repeats), axis, split_axis=dim, concat_axis=di...]
    all_gather x1 -> x0, waiting for transfers between devices: 157 us -> none  [local(): all_rows = lax.all_gather(tokens, ('dp', 'depth'), axis=0, tiled=True)]
    all_to_all x0 -> x1, starting transfers between devices: none -> 8.39 us  [tiled_gather(): lax.all_to_all(jnp.tile(x, repeats), axis, split_axis=dim, concat_axis=di...]
    another operation x0 -> x1, local copies, waits for them, and re-layouts: none -> 7.54 us  [tiled_gather(): jnp.tile(x, repeats)]
where the time goes in v1:
time: 475 us
  waiting for transfers between devices  380 us (80%)
  matrix products  59.5 us (13%)
  between operations  14.1 us (3%)
  starting transfers between devices  8.65 us (2%)
  local copies, waits for them, and re-layouts  7.54 us (2%)
  other arithmetic  4.9 us (1%)
    all_to_all x1, waiting for transfers between devices, tiled_gather(): lax.all_to_all(jnp.tile(x, repeats), axis, split_axis=dim, concat_axis=di...  296 us
    all_gather x1, waiting for transfers between devices, local(): lax.all_gather(grad_pre, ('dp', 'grid'), axis=0, tiled=True)  74.2 us
    dot_general x1, matrix products, local(): partial_pre = jnp.dot(own_rows, weight, preferred_element_type=jnp.float32)  31.6 us
    dot_general x1, matrix products, transposed_product(): lax.dot_general(left, right, (((0,), (0,)), ((), ())), preferred_element_...  27.9 us
    reduce_scatter x1, waiting for transfers between devices, local(): lax.psum_scatter(partial_pre, 'grid', scatter_dimension=0, tiled=True)  10.4 us
  transfers between devices with their start and end apart: 3, of which 3 were waited for; matrix products, arithmetic and copies ran while one was open for 0% of the time, Pallas kernels for 0%

profile of v1, /device:TPU:0, one launch (start us, length us, event | category | flops | bytes accessed | tf_op | source)
XLA Modules:
  0.0 474.8 jit_solution(2424387515481224075)
XLA Ops:
  7.2 7.5 %tile.2 = bf16[16,64,6144]{2,1,0:T(8,128)(2,1)} broadcast(bf16[64,6144]{1,0:T(8,128)(2,1)} %param.3), dimensions={1,2} | broadcast | bytes 13369344 | tf_op jit(solution)/shard_map/tile | solution.py:10
  14.7 8.4 %all-to-all-start = ((bf16[16,64,6144]{2,1,0:T(8,128)(2,1)}), bf16[16,64,6144]{2,1,0:T(8,128)(2,1)}, u32[]{:S(2)}, u32[]{:S(2)}) async-start(bf16[16,64,6144]{2,1,0:T(8,128)(2,1)} %tile.2), calls=%async_computation | async-start | bytes 25165824 | tf_op jit(solution)/shard_map/all_to_all | solution.py:10
  23.1 0.0 reduce-scatter.2.cloned.1.call-start
  23.1 295.6 %all-to-all-done = bf16[16,64,6144]{2,1,0:T(8,128)(2,1)} async-done(((bf16[16,64,6144]{2,1,0:T(8,128)(2,1)}), bf16[16,64,6144]{2,1,0:T(8,128)(2,1)}, u32[]{:S(2)}, u32[]{:S(2)}) %all-to-all-start) | async-done | bytes 12582944 | tf_op jit(solution)/shard_map/all_to_all | solution.py:10
  318.7 31.6 %fusion.11 = f32[256,6144]{1,0:T(8,128)} fusion(bf16[6144,6144]{1,0:T(8,128)(2,1)} %param.4, bf16[1024,6144]{1,0:T(8,128)(2,1)} %bitcast, s32[]{:T(128)S(6)} %select_n.6), kind=kOutput, calls=%fused_computation.17 | convolution fusion | flops 19327352832 | bytes 84934656 | tf_op jit(solution)/shard_map/dot_general | solution.py:27
  350.3 0.0 copy-start
  350.3 0.0 reduce-scatter.2.cloned.1.call-update
  350.3 0.2 all-gather.2.cloned.1.call-start
  350.6 10.4 %reduce-scatter.2.cloned.1.call-done = f32[128,6144]{1,0:T(8,128)} async-done(((f32[256,6144]{1,0:T(8,128)}), f32[128,6144]{1,0:T(8,128)}) %reduce-scatter.2.cloned.1.call-update) | async-done | bytes 3145744 | tf_op jit(solution)/shard_map/reduce_scatter | solution.py:28
  360.9 0.0 copy-done
  360.9 4.9 %fusion.2 = (bf16[128,6144]{1,0:T(8,128)(2,1)}, bf16[128,6144]{1,0:T(8,128)(2,1)}) fusion(bf16[128,6144]{1,0:T(8,128)(2,1)S(1)} %copy-done, f32[128,6144]{1,0:T(8,128)} %reduce-scatter.2.cloned.1.call-done), kind=kLoop, calls=%fused_computation.7 | loop fusion | flops 18087936 | bytes 7864320 | tf_op jit(solution)/shard_map/convert_element_type | solution.py:31
  365.8 0.0 all-gather.2.cloned.1.call-update
  365.9 74.2 %all-gather.2.cloned.1.call-done = bf16[1024,6144]{1,0:T(8,128)(2,1)} async-done(((bf16[128,6144]{1,0:T(8,128)(2,1)}), bf16[1024,6144]{1,0:T(8,128)(2,1)}) %all-gather.2.cloned.1.call-update) | async-done | bytes 12582928 | tf_op jit(solution)/shard_map/all_gather | solution.py:35
  440.1 27.9 %convolution_convert_fusion = bf16[1536,6144]{1,0:T(8,128)(2,1)} fusion(bf16[1024,6144]{1,0:T(8,128)(2,1)} %all-gather.2.cloned.1.call-done, bf16[1024,6144]{1,0:T(8,128)(2,1)} %bitcast, s32[]{:T(128)S(6)} %select_n.7), kind=kOutput, calls=%fused_computation | convolution fusion | flops 19336790016 | bytes 34603012 | tf_op jit(solution)/shard_map/dot_general | solution.py:18
Async XLA Ops:
  14.7 304.0 %all-to-all-start = ((bf16[16,64,6144]{2,1,0:T(8,128)(2,1)}), bf16[16,64,6144]{2,1,0:T(8,128)(2,1)}, u32[]{:S(2)}, u32[]{:S(2)}) async-start(bf16[16,64,6144]{2,1,0:T(8,128)(2,1)} %tile.2), calls=%async_computation | async-start | bytes 25165824 | tf_op jit(solution)/shard_map/all_to_all | solution.py:10
  23.1 337.8 %reduce-scatter.2.cloned.1.call-start = ((), (), s32[]{:S(2)}) async-start(), calls=%async_computation.2 | async-start | bytes 9437184 | tf_op jit(solution)/shard_map/reduce_scatter | solution.py:28
  350.3 10.6 %copy-start = (bf16[128,6144]{1,0:T(8,128)(2,1)S(1)}, bf16[128,6144]{1,0:T(8,128)(2,1)}, u32[]{:S(2)}) copy-start(bf16[128,6144]{1,0:T(8,128)(2,1)} %param.5) | copy-start | bytes 4718596
  350.3 89.7 %all-gather.2.cloned.1.call-start = ((), (), s32[]{:S(2)}) async-start(), calls=%async_computation.3 | async-start | bytes 14155776 | tf_op jit(solution)/shard_map/all_gather | solution.py:35
Sparse Core Ops, SparseCore 0:
  350.5 10.4 reduce-scatter.1
  366.0 74.0 all-gather.1

commit v2 on v0

--- a/solution.py
+++ b/solution.py
@@ -26,7 +26,13 @@
     sub_width = all_rows.shape[1] // lax.axis_size("dp")
     columns = lax.dynamic_slice_in_dim(all_rows, lax.axis_index("dp") * sub_width, sub_width, 1)
     weight_grad = transposed_product(
-        columns, lax.all_gather(grad_pre, ("dp", "grid"), axis=0, tiled=True)
+        columns,
+        jnp.concatenate(
+            lax.all_to_all(
+                jnp.stack([grad_pre] * lax.axis_size(("dp", "grid"))), ("dp", "grid"), 0, 0
+            ),
+            axis=0,
+        ),
     )
     return (hidden, weight_grad.astype(jnp.bfloat16))
 

time: 323 us -> 400 us (1.24)
  waiting for transfers between devices: 244 us -> 309 us
  local copies, waits for them, and re-layouts: 0.01 us -> 6.49 us
  starting transfers between devices: 0.12 us -> 5.62 us
    all_to_all x0 -> x1, waiting for transfers between devices: none -> 139 us  [local(): lax.all_to_all(jnp.stack([grad_pre] * lax.axis_size(('dp', 'grid'))), ('d...]
    all_gather x1 -> x0, waiting for transfers between devices: 74.2 us -> none  [local(): lax.all_gather(grad_pre, ('dp', 'grid'), axis=0, tiled=True)]
    another operation x0 -> x1, local copies, waits for them, and re-layouts: none -> 6.49 us  [local(): jnp.stack([grad_pre] * lax.axis_size(('dp', 'grid')))]
    all_to_all x0 -> x1, starting transfers between devices: none -> 5.55 us  [local(): lax.all_to_all(jnp.stack([grad_pre] * lax.axis_size(('dp', 'grid'))), ('d...]
where the time goes in v2:
time: 400 us; the launch traced here: 399 us
  waiting for transfers between devices  309 us (77%)
  matrix products  59.5 us (15%)
  between operations  14.1 us (4%)
  local copies, waits for them, and re-layouts  6.49 us (2%)
  starting transfers between devices  5.62 us (1%)
  other arithmetic  4.64 us (1%)
    all_gather x1, waiting for transfers between devices, local(): all_rows = lax.all_gather(tokens, ('dp', 'depth'), axis=0, tiled=True)  157 us
    all_to_all x1, waiting for transfers between devices, local(): lax.all_to_all(jnp.stack([grad_pre] * lax.axis_size(('dp', 'grid'))), ('d...  139 us
    dot_general x1, matrix products, local(): partial_pre = jnp.dot(own_rows, weight, preferred_element_type=jnp.float32)  31.6 us
    dot_general x1, matrix products, transposed_product(): lax.dot_general(left, right, (((0,), (0,)), ((), ())), preferred_element_...  27.9 us
    reduce_scatter x1, waiting for transfers between devices, local(): lax.psum_scatter(partial_pre, 'grid', scatter_dimension=0, tiled=True)  12.4 us
  transfers between devices with their start and end apart: 3, of which 3 were waited for; matrix products, arithmetic and copies ran while one was open for 0% of the time, Pallas kernels for 0%

profile of v2, /device:TPU:0, one launch (start us, length us, event | category | flops | bytes accessed | tf_op | source)
XLA Modules:
  0.0 399.3 jit_solution(507528476470847802)
XLA Ops:
  7.2 0.0 all-gather.2.cloned.1.call-start
  7.2 0.7 all-gather.2.cloned.1.call-update
  7.9 0.0 reduce-scatter.2.cloned.1.call-start
  7.9 157.1 %all-gather.2.cloned.1.call-done = bf16[1024,6144]{1,0:T(8,128)(2,1)} async-done(((bf16[64,6144]{1,0:T(8,128)(2,1)}), bf16[1024,6144]{1,0:T(8,128)(2,1)}) %all-gather.2.cloned.1.call-update) | async-done | bytes 12582928 | tf_op jit(solution)/shard_map/all_gather | solution.py:18
  165.0 31.6 %fusion.11 = f32[256,6144]{1,0:T(8,128)} fusion(bf16[6144,6144]{1,0:T(8,128)(2,1)} %param.4, bf16[1024,6144]{1,0:T(8,128)(2,1)} %all-gather.2.cloned.1.call-done, s32[]{:T(128)S(6)} %select_n.6), kind=kOutput, calls=%fused_computation.17 | convolution fusion | flops 19327352832 | bytes 84934656 | tf_op jit(solution)/shard_map/dot_general | solution.py:21
  196.6 0.0 copy-start
  196.6 0.0 reduce-scatter.2.cloned.1.call-update
  196.6 12.4 %reduce-scatter.2.cloned.1.call-done = f32[128,6144]{1,0:T(8,128)} async-done(((f32[256,6144]{1,0:T(8,128)}), f32[128,6144]{1,0:T(8,128)}) %reduce-scatter.2.cloned.1.call-update) | async-done | bytes 3145744 | tf_op jit(solution)/shard_map/reduce_scatter | solution.py:22
  209.0 0.0 copy-done
  209.0 4.6 %fusion.2 = (bf16[128,6144]{1,0:T(8,128)(2,1)S(1)}, bf16[128,6144]{1,0:T(8,128)(2,1)}) fusion(bf16[128,6144]{1,0:T(8,128)(2,1)S(1)} %copy-done, f32[128,6144]{1,0:T(8,128)} %reduce-scatter.2.cloned.1.call-done), kind=kLoop, calls=%fused_computation.7 | loop fusion | flops 18087936 | bytes 7864320 | tf_op jit(solution)/shard_map/convert_element_type | solution.py:25
  213.7 6.5 %stack.2 = bf16[8,128,6144]{2,1,0:T(8,128)(2,1)} broadcast(bf16[128,6144]{1,0:T(8,128)(2,1)S(1)} %get-tuple-element.2), dimensions={1,2} | broadcast | bytes 14155776 | tf_op jit(solution)/shard_map/stack | solution.py:32
  220.2 5.5 %all-to-all-start = ((bf16[8,128,6144]{2,1,0:T(8,128)(2,1)}), bf16[8,128,6144]{2,1,0:T(8,128)(2,1)}, u32[]{:S(2)}, u32[]{:S(2)}) async-start(bf16[8,128,6144]{2,1,0:T(8,128)(2,1)} %stack.2), calls=%async_computation.1 | async-start | bytes 25165824 | tf_op jit(solution)/shard_map/all_to_all | solution.py:31
  225.7 138.8 %all-to-all-done = bf16[8,128,6144]{2,1,0:T(8,128)(2,1)} async-done(((bf16[8,128,6144]{2,1,0:T(8,128)(2,1)}), bf16[8,128,6144]{2,1,0:T(8,128)(2,1)}, u32[]{:S(2)}, u32[]{:S(2)}) %all-to-all-start) | async-done | bytes 12582944 | tf_op jit(solution)/shard_map/all_to_all | solution.py:31
  364.6 27.9 %convolution_convert_fusion = bf16[1536,6144]{1,0:T(8,128)(2,1)} fusion(bf16[1024,6144]{1,0:T(8,128)(2,1)} %bitcast, bf16[1024,6144]{1,0:T(8,128)(2,1)} %all-gather.2.cloned.1.call-done, s32[]{:T(128)S(6)} %select_n.7), kind=kOutput, calls=%fused_computation | convolution fusion | flops 19336790016 | bytes 34603012 | tf_op jit(solution)/shard_map/dot_general | solution.py:12
Async XLA Ops:
  7.2 157.8 %all-gather.2.cloned.1.call-start = ((), (), s32[]{:S(2)}) async-start(), calls=%async_computation.2 | async-start | bytes 13369344 | tf_op jit(solution)/shard_map/all_gather | solution.py:18
  7.9 201.1 %reduce-scatter.2.cloned.1.call-start = ((), (), s32[]{:S(2)}) async-start(), calls=%async_computation.3 | async-start | bytes 9437184 | tf_op jit(solution)/shard_map/reduce_scatter | solution.py:22
  196.6 12.4 %copy-start = (bf16[128,6144]{1,0:T(8,128)(2,1)S(1)}, bf16[128,6144]{1,0:T(8,128)(2,1)}, u32[]{:S(2)}) copy-start(bf16[128,6144]{1,0:T(8,128)(2,1)} %param.5) | copy-start | bytes 4718596
  220.2 144.4 %all-to-all-start = ((bf16[8,128,6144]{2,1,0:T(8,128)(2,1)}), bf16[8,128,6144]{2,1,0:T(8,128)(2,1)}, u32[]{:S(2)}, u32[]{:S(2)}) async-start(bf16[8,128,6144]{2,1,0:T(8,128)(2,1)} %stack.2), calls=%async_computation.1 | async-start | bytes 25165824 | tf_op jit(solution)/shard_map/all_to_all | solution.py:31
Sparse Core Ops, SparseCore 0:
  10.8 154.1 all-gather.1
  196.8 12.2 reduce-scatter.1
